TPU v7x, 32 devices: a whole 2x2x4 slice. The times are simulated.
32 devices in a mesh: groups: 2 (over y), wide: 8 (over z, x), narrow: 2 (over core).
Axes of the slice: x: 2, y: 2, z: 4, core: 2. Of those that a mesh axis runs over, the one named last changes fastest.
Arguments:
- goals: float32 [8192, 1024], P(('groups', 'wide', 'narrow')), parts along dimension 0, may hold values from -32 to 32
- premises: float32 [1024, 1024], P(('groups', 'wide', 'narrow')), parts along dimension 0, may hold values from -24 to 24
- counts: int32 [8192], P(('groups', 'wide')), parts along dimension 0, may hold values from 1 to 16
- positives: int32 [8192, 16], P(('groups', 'wide')), parts along dimension 0, may hold values from -1 to 511, as said below
- cotangent: float32 [8192], P(('groups', 'wide')), parts along dimension 0, may hold values from -6 to 6
Outputs:
- goal_loss: float32 [8192], P(('groups', 'wide')), parts along dimension 0
- grad_goals: float32 [8192, 1024], P(('groups', 'wide', 'narrow')), parts along dimension 0
- grad_premises: float32 [1024, 1024], P(('groups', 'wide', 'narrow')), parts along dimension 0
There are 2 independent parts, one for each index of `groups`. A program takes and returns all parts, laid end to end along the dimension named above; each array names one. Nothing has to cross between parts.
Inputs may be any that keep to these rules, and one draw needn't show every extreme that they name: positives[i, k] is a premise index for k < counts[i] and -1 from there on.
All inputs are finite; a program needn't handle non-finite values.
Results may differ from a plain program's by a relative error of at most 0.012.
The roundings to bfloat16 on the way count: a program that leaves them out, or rounds other values in their place, can miss the bound.
Values may be sent and summed in bfloat16 or wider, within the bound.
A program may use at most 64 MiB of HBM per device.

v0:
```python
import jax
import jax.numpy as jnp
from jax import lax
from jax.sharding import PartitionSpec as P


def hit_counts(row_lists, column_ids):
    total = jnp.zeros((row_lists.shape[0], column_ids.shape[0]), jnp.float32)
    for which_slot in range(row_lists.shape[1]):
        total = total + (row_lists[:, which_slot][:, None] == column_ids[None, :]).astype(
            jnp.float32
        )
    return total


def per_device(goals, premises, counts, positives, cotangent):
    goal_part = goals.astype(jnp.bfloat16)
    prem_part = premises.astype(jnp.bfloat16)
    prem_rows = prem_part.shape[0]
    width = goal_part.shape[1]
    scale = width ** (-0.5)
    n_wide = lax.axis_size("wide")
    n_narrow = lax.axis_size("narrow")
    narrow_index = lax.axis_index("narrow")
    rows_block = lax.all_gather(goal_part, "narrow", axis=0, tiled=True)
    prem_block = lax.all_gather(prem_part, "wide", axis=0, tiled=True)
    goal_counts = counts.astype(jnp.float32)
    local_ids = jnp.arange(prem_rows * n_wide, dtype=jnp.int32)
    column_ids = (
        local_ids // prem_rows * n_narrow + narrow_index
    ) * prem_rows + local_ids % prem_rows
    col_total = prem_block.shape[0]
    row_total = rows_block.shape[0]
    step_cols = 512 if col_total % 512 == 0 else col_total
    starts = list(range(0, col_total, step_cols))

    def tile_scores(begin):
        piece = prem_block[begin : begin + step_cols]
        return (
            lax.dot_general(
                rows_block, piece, (((1,), (1,)), ((), ())), preferred_element_type=jnp.float32
            )
            * scale
        )

    top = jnp.full((row_total,), -jnp.inf, jnp.float32)
    total = jnp.zeros((row_total,), jnp.float32)
    positive_sum = jnp.zeros((row_total,), jnp.float32)
    for begin in starts:
        scores = tile_scores(begin)
        hits = hit_counts(positives, column_ids[begin : begin + step_cols])
        new_top = jnp.maximum(top, jnp.max(scores, axis=1))
        total = total * jnp.exp(top - new_top) + jnp.sum(jnp.exp(scores - new_top[:, None]), axis=1)
        positive_sum = positive_sum + jnp.sum(hits * scores, axis=1)
        top = new_top
    best = lax.pmax(top, "narrow")
    total_all, positive_all = lax.psum((total * jnp.exp(top - best), positive_sum), "narrow")
    log_total = best + jnp.log(total_all)
    row_loss = log_total - positive_all / goal_counts
    grad_rows = jnp.zeros((row_total, width), jnp.float32)
    pieces = []
    for number, begin in enumerate(starts):
        scores = tile_scores(begin)
        hits = hit_counts(positives, column_ids[begin : begin + step_cols])
        dscores = (
            cotangent[:, None]
            * (jnp.exp(scores - log_total[:, None]) - hits / goal_counts[:, None])
            * scale
        ).astype(jnp.bfloat16)
        grad_rows = grad_rows + jnp.dot(
            dscores, prem_block[begin : begin + step_cols], preferred_element_type=jnp.float32
        )
        pieces.append(dscores)
    stored = jnp.concatenate(pieces, axis=1)
    grad_goals = lax.psum_scatter(grad_rows, "narrow", scatter_dimension=0, tiled=True)
    grad_premises = lax.psum_scatter(
        lax.dot_general(
            stored, rows_block, (((0,), (0,)), ((), ())), preferred_element_type=jnp.float32
        ),
        "wide",
        scatter_dimension=0,
        tiled=True,
    )
    return (row_loss, grad_goals, grad_premises)


def solution(mesh):
    return jax.shard_map(
        per_device,
        mesh=mesh,
        in_specs=(
            P(("groups", "wide", "narrow"), None),
            P(("groups", "wide", "narrow"), None),
            P(("groups", "wide")),
            P(("groups", "wide"), None),
            P(("groups", "wide")),
        ),
        out_specs=(
            P(("groups", "wide")),
            P(("groups", "wide", "narrow"), None),
            P(("groups", "wide", "narrow"), None),
        ),
        check_vma=False,
    )
```

profile of v0, /device:TPU:0, one launch (start us, length us, event | category | flops | bytes accessed | tf_op | source)
XLA Modules:
  0.0 136.1 jit_solution(13301415830657365863)
XLA Ops:
  7.2 0.0 copy-start.2
  7.2 0.0 copy-start
  7.2 0.0 copy-start.1
  7.2 0.0 all-gather.2.cloned.1.call-start
  7.2 2.1 %convert_element_type.76 = bf16[256,1024]{1,0:T(8,128)(2,1)} convert(f32[256,1024]{1,0:T(8,128)} %param.5) | non-fusion elementwise | flops 262144 | bytes 1572864 | tf_op jit(solution)/shard_map/convert_element_type | solution.py:17
  9.4 0.0 copy-start.4
  9.4 0.0 all-gather.2.cloned.1.call-update
  9.4 0.0 reduce-scatter.5.cloned.1.call-start
  9.4 0.0 copy-done.2
  9.5 0.0 copy-done
  9.5 0.0 copy-done.1
  9.6 33.0 %all_gather.7 = bf16[256,1024]{1,0:T(8,128)(2,1)S(1)} all-gather(bf16[32,1024]{1,0:T(8,128)(2,1)S(1)} %convert_element_type.77), channel_id=1, replica_groups=mesh['groups'=2,'wide'=8,'narrow'=2] {'wide'}, dimensions={0}, use_global_device_ids=true | all-gather | bytes 589824 | tf_op jit(solution)/shard_map/all_gather | solution.py:26
  42.6 0.0 all-gather.2.cloned.1.call-done
  42.6 0.0 copy-start.3
  42.6 1.8 %fusion.9 = (f32[512]{0:T(512)S(1)}, f32[512,256]{0,1:T(8,128)S(1)}) fusion(bf16[512,1024]{1,0:T(8,128)(2,1)} %all-gather.2.cloned.1.call-done, bf16[256,1024]{1,0:T(8,128)(2,1)S(1)} %all_gather.7), kind=kOutput, calls=%fused_computation.22 | convolution fusion | flops 268697088 | bytes 2099200 | tf_op jit(solution)/shard_map/dot_general | solution.py:40
  44.4 2.5 %pmax.7 = f32[512]{0:T(512)S(1)} all-reduce(f32[512]{0:T(512)S(1)} %get-tuple-element.25), channel_id=1, replica_groups=mesh['groups'=2,'wide'=8,'narrow'=2] {'narrow'}, use_global_device_ids=true, to_apply=%region_1.2 | all-reduce | flops 512 | bytes 4096 | tf_op jit(solution)/shard_map/pmax | solution.py:56
  46.9 1.1 multiply_reduce_fusion
  47.9 2.5 %all-reduce = (f32[512]{0:T(512)S(1)}, f32[512]{0:T(512)S(1)}) all-reduce(f32[512]{0:T(512)S(1)} %exponential_multiply_fusion, f32[512]{0:T(512)S(1)} %get-tuple-element.3), channel_id=1, replica_groups=mesh['groups'=2,'wide'=8,'narrow'=2] {'narrow'}, use_global_device_ids=true, to_apply=%region_3.4 | all-reduce | flops 1024 | bytes 8192 | tf_op jit(solution)/shard_map/psum | solution.py:57
  50.4 0.6 divide_subtract_fusion
  51.0 0.0 copy-done.4
  51.0 0.0 copy-done.3
  51.0 2.3 %fusion.6 = f32[256,1024]{1,0:T(8,128)} fusion(bf16[512,1024]{1,0:T(8,128)(2,1)S(1)} %copy-done.3, f32[512,256]{0,1:T(8,128)S(1)} %get-tuple-element.26, f32[512]{0:T(512)S(1)} %convert_element_type.94, f32[512]{0:T(512)S(1)} %get-tuple-element.8, f32[512]{0:T(512)S(1)} %copy-done.4, s32[512]{0:T(512)S(1)} %bitcast.63, s32[512]{0:T(512)S(1)} %bitcast.66, ...), kind=kOutput, calls=%fused_computation.19 | convolution fusion | flops 275382272 | bytes 2661376 | tf_op jit(solution)/shard_map/dot_general | solution.py:77
  53.3 0.0 reduce-scatter.5.cloned.1.call-update
  53.3 0.0 reduce-scatter.3.cloned.1.call-start
  53.4 2.7 %fusion.7 = f32[512,1024]{1,0:T(8,128)} fusion(bf16[256,1024]{1,0:T(8,128)(2,1)S(1)} %all_gather.7, f32[512,256]{0,1:T(8,128)S(1)} %get-tuple-element.26, f32[512]{0:T(512)S(1)} %convert_element_type.94, f32[512]{0:T(512)S(1)} %get-tuple-element.8, f32[512]{0:T(512)S(1)} %copy-done.4, s32[512]{0:T(512)S(1)} %bitcast.64, s32[512]{0:T(512)S(1)} %bitcast.67, ...), kind=kOutput, calls=%fused_computation.20 | convolution fusion | flops 275382272 | bytes 3185664 | tf_op jit(solution)/shard_map/dot_general | solution.py:70
  56.1 0.0 reduce-scatter.3.cloned.1.call-update
  56.1 61.9 %reduce-scatter.5.cloned.1.call-done = f32[32,1024]{1,0:T(8,128)} async-done(((f32[256,1024]{1,0:T(8,128)}), f32[32,1024]{1,0:T(8,128)}) %reduce-scatter.5.cloned.1.call-update) | async-done | bytes 131088 | tf_op jit(solution)/shard_map/reduce_scatter | solution.py:76
  118.0 11.6 %reduce-scatter.3.cloned.1.call-done = f32[256,1024]{1,0:T(8,128)} async-done(((f32[512,1024]{1,0:T(8,128)}), f32[256,1024]{1,0:T(8,128)}) %reduce-scatter.3.cloned.1.call-update) | async-done | bytes 1048592 | tf_op jit(solution)/shard_map/reduce_scatter | solution.py:75
  (5 shorter events, 0.1 us)
Async XLA Ops:
  7.2 2.3 %copy-start.2 = (s32[512]{0:T(512)S(1)}, s32[512]{0:T(512)}, u32[]{:S(2)}) copy-start(s32[512]{0:T(512)} %param.7) | copy-start | bytes 6148
  7.2 2.3 %copy-start = (f32[32,1024]{1,0:T(8,128)S(1)}, f32[32,1024]{1,0:T(8,128)}, u32[]{:S(2)}) copy-start(f32[32,1024]{1,0:T(8,128)} %param.6) | copy-start | bytes 393220
  7.2 2.3 %copy-start.1 = (s32[512,16]{0,1:T(8,128)S(1)}, s32[512,16]{0,1:T(8,128)}, u32[]{:S(2)}) copy-start(s32[512,16]{0,1:T(8,128)} %param.8) | copy-start | bytes 98308
  7.2 35.4 %all-gather.2.cloned.1.call-start = ((), (), s32[]{:S(2)}) async-start(), calls=%async_computation.2 | async-start | bytes 1572864 | tf_op jit(solution)/shard_map/all_gather | solution.py:25
  9.4 41.6 %copy-start.4 = (f32[512]{0:T(512)S(1)}, f32[512]{0:T(512)}, u32[]{:S(2)}) copy-start(f32[512]{0:T(512)} %param.9) | copy-start | bytes 6148
  9.4 108.6 %reduce-scatter.5.cloned.1.call-start = ((), (), s32[]{:S(2)}) async-start(), calls=%async_computation.4 | async-start | bytes 1179648 | tf_op jit(solution)/shard_map/reduce_scatter | solution.py:76
  42.6 8.4 %copy-start.3 = (bf16[512,1024]{1,0:T(8,128)(2,1)S(1)}, bf16[512,1024]{1,0:T(8,128)(2,1)}, u32[]{:S(2)}) copy-start(bf16[512,1024]{1,0:T(8,128)(2,1)} %all-gather.2.cloned.1.call-done) | copy-start | bytes 3145732
  53.3 76.3 %reduce-scatter.3.cloned.1.call-start = ((), (), s32[]{:S(2)}) async-start(), calls=%async_computation.3 | async-start | bytes 3145728 | tf_op jit(solution)/shard_map/reduce_scatter | solution.py:75
Sparse Core Ops, SparseCore 0:
  10.1 11.7 all-gather.1
  53.4 64.5 reduce-scatter.4
  120.9 8.6 reduce-scatter.2
where the time goes:
time: 136 us
  waiting for transfers between devices  73.5 us (54%)
  blocking collectives  38 us (28%)
  between operations  13.8 us (10%)
  matrix products  6.82 us (5%)
  other arithmetic  3.82 us (3%)
    reduce_scatter x1, waiting for transfers between devices, per_device(): lax.psum_scatter(lax.dot_general(stored, rows_block, (((0,), (0,)), ((),...  61.9 us
    all_gather x1, blocking collectives, per_device(): prem_block = lax.all_gather(prem_part, 'wide', axis=0, tiled=True)  33 us
    reduce_scatter x1, waiting for transfers between devices, per_device(): lax.psum_scatter(grad_rows, 'narrow', scatter_dimension=0, tiled=True)  11.6 us
    dot_general x1, matrix products, per_device(): jnp.dot(dscores, prem_block[begin:begin + step_cols], preferred_element_t...  2.73 us
  transfers between devices with their start and end apart: 3, of which 2 were waited for; matrix products, arithmetic and copies ran while one was open for 2% of the time, Pallas kernels for 0%

commit v1 on v0

--- a/solution.py
+++ b/solution.py
@@ -23,7 +23,26 @@
     n_narrow = lax.axis_size("narrow")
     narrow_index = lax.axis_index("narrow")
     rows_block = lax.all_gather(goal_part, "narrow", axis=0, tiled=True)
-    prem_block = lax.all_gather(prem_part, "wide", axis=0, tiled=True)
+    length, index, span = (lax.axis_size("wide"), lax.axis_index("wide"), prem_part.shape[0])
+    right = [(i, (i + 1) % length) for i in range(length)]
+    left = [(i, (i - 1) % length) for i in range(length)]
+    filled = jnp.zeros(
+        (*prem_part.shape[:0], length * span, *prem_part.shape[0 + 1 :]), prem_part.dtype
+    )
+    filled = lax.dynamic_update_slice_in_dim(filled, prem_part, index * span, axis=0)
+    from_left = from_right = prem_part
+    half = length // 2
+    for step in range(1, half + 1):
+        from_left = lax.ppermute(from_left, "wide", right)
+        filled = lax.dynamic_update_slice_in_dim(
+            filled, from_left, (index - step) % length * span, axis=0
+        )
+        if step < length - half:
+            from_right = lax.ppermute(from_right, "wide", left)
+            filled = lax.dynamic_update_slice_in_dim(
+                filled, from_right, (index + step) % length * span, axis=0
+            )
+    prem_block = filled
     goal_counts = counts.astype(jnp.float32)
     local_ids = jnp.arange(prem_rows * n_wide, dtype=jnp.int32)
     column_ids = (

time: 136 us -> 128 us (0.941)
  blocking collectives: 38 us -> 4.94 us
  starting transfers between devices: 0.12 us -> 15.6 us
  waiting for transfers between devices: 73.5 us -> 81.3 us
    all_gather x1 -> x0, blocking collectives: 33 us -> none  [per_device(): prem_block = lax.all_gather(prem_part, 'wide', axis=0, tiled=True)]
    ppermute x0 -> x7, starting transfers between devices: none -> 15.5 us  [the longest x3 12.5 us: per_device(): from_right = lax.ppermute(from_right, 'wide', left)]
    ppermute x0 -> x7, waiting for transfers between devices: none -> 11.4 us  [the longest x4 11.3 us: per_device(): from_left = lax.ppermute(from_left, 'wide', right)]
    reduce_scatter x1, waiting for transfers between devices: 61.9 us -> 58.2 us  [per_device(): lax.psum_scatter(lax.dot_general(stored, rows_block, (((0,), (0,)), ((),...]
  transfers between devices with their start and end apart: 3 -> 10, of which waited for: 2 -> 6; matrix products, arithmetic and copies ran while one was open for 2% -> 4% of each run, Pallas kernels for 0% -> 0%
where the time goes in v1:
time: 128 us
  waiting for transfers between devices  81.3 us (64%)
  starting transfers between devices  15.6 us (12%)
  between operations  14.1 us (11%)
  matrix products  6.8 us (5%)
  blocking collectives  4.94 us (4%)
  other arithmetic  4.71 us (4%)
    reduce_scatter x1, waiting for transfers between devices, per_device(): lax.psum_scatter(lax.dot_general(stored, rows_block, (((0,), (0,)), ((),...  58.2 us
    ppermute x3, starting transfers between devices, per_device(): from_right = lax.ppermute(from_right, 'wide', left)  12.5 us
    reduce_scatter x1, waiting for transfers between devices, per_device(): lax.psum_scatter(grad_rows, 'narrow', scatter_dimension=0, tiled=True)  11.6 us
    ppermute x4, waiting for transfers between devices, per_device(): from_left = lax.ppermute(from_left, 'wide', right)  11.3 us
    ppermute x4, starting transfers between devices, per_device(): from_left = lax.ppermute(from_left, 'wide', right)  3.05 us
    dot_general x1, matrix products, per_device(): jnp.dot(dscores, prem_block[begin:begin + step_cols], preferred_element_t...  2.72 us
  transfers between devices with their start and end apart: 10, of which 6 were waited for; matrix products, arithmetic and copies ran while one was open for 4% of the time, Pallas kernels for 0%

profile of v1, /device:TPU:0, one launch (start us, length us, event | category | flops | bytes accessed | tf_op | source)
XLA Modules:
  0.0 127.6 jit_solution(5284921674256027413)
XLA Ops:
  7.2 0.0 all-gather.2.cloned.1.call-start
  7.2 0.1 broadcast_in_dim.6
  7.3 0.9 constant_dynamic-update-slice_fusion.7
  8.2 3.0 %collective-permute-start = (bf16[32,1024]{1,0:T(8,128)(2,1)S(1)}, bf16[32,1024]{1,0:T(8,128)(2,1)S(1)}, u32[]{:S(2)}, u32[]{:S(2)}) collective-permute-start(bf16[32,1024]{1,0:T(8,128)(2,1)S(1)} %get-tuple-element.10), channel_id=1, source_target_pairs={{0,2},{2,4},{4,6},{6,8},{8,10},{10,12},{12,14},{14,0},{1,3},{3,5},... | collective-permute-start | bytes 196616 | tf_op jit(solution)/shard_map/ppermute | solution.py:36
  11.2 3.1 %collective-permute-start.1 = (bf16[32,1024]{1,0:T(8,128)(2,1)S(1)}, bf16[32,1024]{1,0:T(8,128)(2,1)S(1)}, u32[]{:S(2)}, u32[]{:S(2)}) collective-permute-start(bf16[32,1024]{1,0:T(8,128)(2,1)S(1)} %get-tuple-element.10), channel_id=1, source_target_pairs={{0,14},{2,0},{4,2},{6,4},{8,6},{10,8},{12,10},{14,12},{1,15},{3,1}... | collective-permute-start | bytes 196616 | tf_op jit(solution)/shard_map/ppermute | solution.py:41
  14.3 2.1 %convert_element_type.77 = bf16[256,1024]{1,0:T(8,128)(2,1)} convert(f32[256,1024]{1,0:T(8,128)} %param.5) | non-fusion elementwise | flops 262144 | bytes 1572864 | tf_op jit(solution)/shard_map/convert_element_type | solution.py:17
  16.4 0.0 all-gather.2.cloned.1.call-update
  16.4 0.0 copy-start.3
  16.4 0.0 reduce-scatter.5.cloned.1.call-start
  16.7 0.0 collective-permute-done
  16.8 0.1 collective-permute-start.2
  16.8 0.1 collective-permute-done.1
  16.9 4.6 %collective-permute-start.3 = (bf16[32,1024]{1,0:T(8,128)(2,1)S(1)}, bf16[32,1024]{1,0:T(8,128)(2,1)S(1)}, u32[]{:S(2)}, u32[]{:S(2)}) collective-permute-start(bf16[32,1024]{1,0:T(8,128)(2,1)S(1)} %collective-permute-done.1), channel_id=1, source_target_pairs={{0,14},{2,0},{4,2},{6,4},{8,6},{10,8},{12,10},{14,12},{1,15},{3,1}... | collective-permute-start | bytes 196616 | tf_op jit(solution)/shard_map/ppermute | solution.py:41
  21.6 2.2 %collective-permute-done.2 = bf16[32,1024]{1,0:T(8,128)(2,1)S(1)} collective-permute-done((bf16[32,1024]{1,0:T(8,128)(2,1)S(1)}, bf16[32,1024]{1,0:T(8,128)(2,1)S(1)}, u32[]{:S(2)}, u32[]{:S(2)}) %collective-permute-start.2) | collective-permute-done | bytes 65568 | tf_op jit(solution)/shard_map/ppermute | solution.py:36
  23.8 0.0 collective-permute-start.4
  23.8 4.7 %collective-permute-start.5 = (bf16[32,1024]{1,0:T(8,128)(2,1)S(1)}, bf16[32,1024]{1,0:T(8,128)(2,1)S(1)}, u32[]{:S(2)}, u32[]{:S(2)}) collective-permute-start(bf16[32,1024]{1,0:T(8,128)(2,1)S(1)} %collective-permute-done.3), channel_id=1, source_target_pairs={{0,14},{2,0},{4,2},{6,4},{8,6},{10,8},{12,10},{14,12},{1,15},{3,1}... | collective-permute-start | bytes 196616 | tf_op jit(solution)/shard_map/ppermute | solution.py:41
  28.5 2.2 %collective-permute-done.4 = bf16[32,1024]{1,0:T(8,128)(2,1)S(1)} collective-permute-done((bf16[32,1024]{1,0:T(8,128)(2,1)S(1)}, bf16[32,1024]{1,0:T(8,128)(2,1)S(1)}, u32[]{:S(2)}, u32[]{:S(2)}) %collective-permute-start.4) | collective-permute-done | bytes 65568 | tf_op jit(solution)/shard_map/ppermute | solution.py:36
  30.7 0.0 collective-permute-done.5
  30.8 6.9 %collective-permute-done.6 = bf16[32,1024]{1,0:T(8,128)(2,1)S(1)} collective-permute-done((bf16[32,1024]{1,0:T(8,128)(2,1)S(1)}, bf16[32,1024]{1,0:T(8,128)(2,1)S(1)}, u32[]{:S(2)}, u32[]{:S(2)}) %collective-permute-start.6) | collective-permute-done | bytes 65568 | tf_op jit(solution)/shard_map/ppermute | solution.py:36
  37.7 0.0 all-gather.2.cloned.1.call-done
  37.7 1.8 %fusion.19 = (f32[512]{0:T(512)S(1)}, f32[256,512]{1,0:T(8,128)S(1)}) fusion(bf16[256,1024]{1,0:T(8,128)(2,1)S(1)} %constant_dynamic-update-slice_fusion, bf16[512,1024]{1,0:T(8,128)(2,1)} %all-gather.2.cloned.1.call-done), kind=kOutput, calls=%fused_computation.38 | convolution fusion | flops 268697088 | bytes 2099200 | tf_op jit(solution)/shard_map/dot_general | solution.py:59
  39.6 2.5 %pmax.7 = f32[512]{0:T(512)S(1)} all-reduce(f32[512]{0:T(512)S(1)} %get-tuple-element.27), channel_id=1, replica_groups=mesh['groups'=2,'wide'=8,'narrow'=2] {'narrow'}, use_global_device_ids=true, to_apply=%region_1.2 | all-reduce | flops 512 | bytes 4096 | tf_op jit(solution)/shard_map/pmax | solution.py:75
  42.0 1.1 fusion.2
  43.1 2.5 %all-reduce = (f32[512]{0:T(512)S(1)}, f32[512]{0:T(512)S(1)}) all-reduce(f32[512]{0:T(512)S(1)} %exponential_multiply_fusion, f32[512]{0:T(512)S(1)} %get-tuple-element.3), channel_id=1, replica_groups=mesh['groups'=2,'wide'=8,'narrow'=2] {'narrow'}, use_global_device_ids=true, to_apply=%region_3.4 | all-reduce | flops 1024 | bytes 8192 | tf_op jit(solution)/shard_map/psum | solution.py:76
  45.6 0.6 divide_subtract_fusion
  46.2 2.3 %fusion.14 = f32[256,1024]{1,0:T(8,128)} fusion(bf16[512,1024]{1,0:T(8,128)(2,1)S(1)} %copy-done, f32[256,512]{1,0:T(8,128)S(1)} %get-tuple-element.28, f32[512]{0:T(512)S(1)} %convert_element_type.94, f32[512]{0:T(512)S(1)} %get-tuple-element.8, f32[512]{0:T(512)S(1)} %copy-done.3, s32[512]{0:T(512)S(1)} %bitcast.85, s32[512]{0:T(512)S(1)} %bitcast.88, ...), kind=kOutput, calls=%fused_computation.35 | convolution fusion | flops 275382272 | bytes 2661376 | tf_op jit(solution)/shard_map/dot_general | solution.py:96
  48.5 0.0 reduce-scatter.5.cloned.1.call-update
  48.5 0.0 reduce-scatter.3.cloned.1.call-start
  48.5 2.7 %fusion.16 = f32[512,1024]{1,0:T(8,128)} fusion(bf16[256,1024]{1,0:T(8,128)(2,1)S(1)} %constant_dynamic-update-slice_fusion, f32[256,512]{1,0:T(8,128)S(1)} %get-tuple-element.28, f32[512]{0:T(512)S(1)} %convert_element_type.94, f32[512]{0:T(512)S(1)} %get-tuple-element.8, f32[512]{0:T(512)S(1)} %copy-done.3, s32[512]{0:T(512)S(1)} %bitcast.86, ...), kind=kOutput, calls=%fused_computation.36 | convolution fusion | flops 275382272 | bytes 3185664 | tf_op jit(solution)/shard_map/dot_general | solution.py:89
  51.3 0.0 reduce-scatter.3.cloned.1.call-update
  51.3 58.2 %reduce-scatter.5.cloned.1.call-done = f32[32,1024]{1,0:T(8,128)} async-done(((f32[256,1024]{1,0:T(8,128)}), f32[32,1024]{1,0:T(8,128)}) %reduce-scatter.5.cloned.1.call-update) | async-done | bytes 131088 | tf_op jit(solution)/shard_map/reduce_scatter | solution.py:95
  109.5 11.6 %reduce-scatter.3.cloned.1.call-done = f32[256,1024]{1,0:T(8,128)} async-done(((f32[512,1024]{1,0:T(8,128)}), f32[256,1024]{1,0:T(8,128)}) %reduce-scatter.3.cloned.1.call-update) | async-done | bytes 1048592 | tf_op jit(solution)/shard_map/reduce_scatter | solution.py:94
  (20 shorter events, 0.1 us)
Async XLA Ops:
  7.2 9.5 %copy-start.2 = (s32[512]{0:T(512)S(1)}, s32[512]{0:T(512)}, u32[]{:S(2)}) copy-start(s32[512]{0:T(512)} %param.7) | copy-start | bytes 6148
  7.2 9.5 %copy-start.1 = (s32[512,16]{0,1:T(8,128)S(1)}, s32[512,16]{0,1:T(8,128)}, u32[]{:S(2)}) copy-start(s32[512,16]{0,1:T(8,128)} %param.8) | copy-start | bytes 98308
  7.2 30.5 %all-gather.2.cloned.1.call-start = ((), (), s32[]{:S(2)}) async-start(), calls=%async_computation.2 | async-start | bytes 1572864 | tf_op jit(solution)/shard_map/all_gather | solution.py:25
  8.2 8.5 %collective-permute-start = (bf16[32,1024]{1,0:T(8,128)(2,1)S(1)}, bf16[32,1024]{1,0:T(8,128)(2,1)S(1)}, u32[]{:S(2)}, u32[]{:S(2)}) collective-permute-start(bf16[32,1024]{1,0:T(8,128)(2,1)S(1)} %get-tuple-element.10), channel_id=1, source_target_pairs={{0,2},{2,4},{4,6},{6,8},{8,10},{10,12},{12,14},{14,0},{1,3},{3,5},... | collective-permute-start | bytes 196616 | tf_op jit(solution)/shard_map/ppermute | solution.py:36
  11.2 5.7 %collective-permute-start.1 = (bf16[32,1024]{1,0:T(8,128)(2,1)S(1)}, bf16[32,1024]{1,0:T(8,128)(2,1)S(1)}, u32[]{:S(2)}, u32[]{:S(2)}) collective-permute-start(bf16[32,1024]{1,0:T(8,128)(2,1)S(1)} %get-tuple-element.10), channel_id=1, source_target_pairs={{0,14},{2,0},{4,2},{6,4},{8,6},{10,8},{12,10},{14,12},{1,15},{3,1}... | collective-permute-start | bytes 196616 | tf_op jit(solution)/shard_map/ppermute | solution.py:41
  16.4 29.7 %copy-start.3 = (f32[512]{0:T(512)S(1)}, f32[512]{0:T(512)}, u32[]{:S(2)}) copy-start(f32[512]{0:T(512)} %param.9) | copy-start | bytes 6148
  16.4 93.1 %reduce-scatter.5.cloned.1.call-start = ((), (), s32[]{:S(2)}) async-start(), calls=%async_computation.4 | async-start | bytes 1179648 | tf_op jit(solution)/shard_map/reduce_scatter | solution.py:95
  16.8 7.0 %collective-permute-start.2 = (bf16[32,1024]{1,0:T(8,128)(2,1)S(1)}, bf16[32,1024]{1,0:T(8,128)(2,1)S(1)}, u32[]{:S(2)}, u32[]{:S(2)}) collective-permute-start(bf16[32,1024]{1,0:T(8,128)(2,1)S(1)} %collective-permute-done), channel_id=1, source_target_pairs={{0,2},{2,4},{4,6},{6,8},{8,10},{10,12},{12,14},{14,0},{1,3},{3,5},... | collective-permute-start | bytes 196616 | tf_op jit(solution)/shard_map/ppermute | solution.py:36
  16.9 6.9 %collective-permute-start.3 = (bf16[32,1024]{1,0:T(8,128)(2,1)S(1)}, bf16[32,1024]{1,0:T(8,128)(2,1)S(1)}, u32[]{:S(2)}, u32[]{:S(2)}) collective-permute-start(bf16[32,1024]{1,0:T(8,128)(2,1)S(1)} %collective-permute-done.1), channel_id=1, source_target_pairs={{0,14},{2,0},{4,2},{6,4},{8,6},{10,8},{12,10},{14,12},{1,15},{3,1}... | collective-permute-start | bytes 196616 | tf_op jit(solution)/shard_map/ppermute | solution.py:41
  23.8 7.0 %collective-permute-start.4 = (bf16[32,1024]{1,0:T(8,128)(2,1)S(1)}, bf16[32,1024]{1,0:T(8,128)(2,1)S(1)}, u32[]{:S(2)}, u32[]{:S(2)}) collective-permute-start(bf16[32,1024]{1,0:T(8,128)(2,1)S(1)} %collective-permute-done.2), channel_id=1, source_target_pairs={{0,2},{2,4},{4,6},{6,8},{8,10},{10,12},{12,14},{14,0},{1,3},{3,5},... | collective-permute-start | bytes 196616 | tf_op jit(solution)/shard_map/ppermute | solution.py:36
  23.8 7.0 %collective-permute-start.5 = (bf16[32,1024]{1,0:T(8,128)(2,1)S(1)}, bf16[32,1024]{1,0:T(8,128)(2,1)S(1)}, u32[]{:S(2)}, u32[]{:S(2)}) collective-permute-start(bf16[32,1024]{1,0:T(8,128)(2,1)S(1)} %collective-permute-done.3), channel_id=1, source_target_pairs={{0,14},{2,0},{4,2},{6,4},{8,6},{10,8},{12,10},{14,12},{1,15},{3,1}... | collective-permute-start | bytes 196616 | tf_op jit(solution)/shard_map/ppermute | solution.py:41
  30.7 7.0 %collective-permute-start.6 = (bf16[32,1024]{1,0:T(8,128)(2,1)S(1)}, bf16[32,1024]{1,0:T(8,128)(2,1)S(1)}, u32[]{:S(2)}, u32[]{:S(2)}) collective-permute-start(bf16[32,1024]{1,0:T(8,128)(2,1)S(1)} %collective-permute-done.4), channel_id=1, source_target_pairs={{0,2},{2,4},{4,6},{6,8},{8,10},{10,12},{12,14},{14,0},{1,3},{3,5},... | collective-permute-start | bytes 196616 | tf_op jit(solution)/shard_map/ppermute | solution.py:36
  37.7 8.4 %copy-start = (bf16[512,1024]{1,0:T(8,128)(2,1)S(1)}, bf16[512,1024]{1,0:T(8,128)(2,1)}, u32[]{:S(2)}) copy-start(bf16[512,1024]{1,0:T(8,128)(2,1)} %all-gather.2.cloned.1.call-done) | copy-start | bytes 3145732
  48.5 72.6 %reduce-scatter.3.cloned.1.call-start = ((), (), s32[]{:S(2)}) async-start(), calls=%async_computation.3 | async-start | bytes 3145728 | tf_op jit(solution)/shard_map/reduce_scatter | solution.py:94
Sparse Core Ops, SparseCore 0:
  16.6 7.7 all-gather.1
  48.6 60.8 reduce-scatter.4
  112.4 8.6 reduce-scatter.2
